TPU v7x, 32 devices: a whole 2x2x4 slice. The times are simulated.
32 devices in a mesh: gx: 8 (over z, core), gy: 4 (over y, x).
Axes of the slice: x: 2, y: 2, z: 4, core: 2. Of those that a mesh axis runs over, the one named last changes fastest.
Arguments:
- density: float32 [128, 192, 128], P('gx', 'gy'), may hold values from -6 to 6
- momenta: float32 [3, 128, 192, 128], P(None, 'gx', 'gy'), may hold values from -6 to 6
- smooth_taps: float32 [33], replicated, may hold values from -1 to 1
- deriv_taps: float32 [33], replicated, may hold values from -1 to 1
- kick_step: float32 [], replicated, may hold values from 0.5 to 1.5
Outputs:
- kicked: float32 [3, 128, 192, 128], P(None, 'gx', 'gy')
All inputs are finite; a program needn't handle non-finite values.
Results may differ from a plain program's by a relative error of at most 0.00007.
Values sent between devices are 32-bit elements; how exact they have to be, the bound alone decides.
No kernel may reach another device: no remote copies, remote signals or barrier semaphores. Data moves between devices by JAX's collectives and lax.ppermute only.
A program may use at most 64 MiB of HBM per device.

v0:
```python
import math
import jax
import jax.numpy as jnp
from jax import lax
from jax.sharding import PartitionSpec as P

FACTOR = 4
LONG_COUPLING = 16.0
HIGHEST = lax.Precision.HIGHEST


def extended(cells, sides, width):
    for axis, dim in sides:
        count = lax.axis_size(axis)
        head = lax.slice_in_dim(cells, 0, width, axis=dim)
        tail = lax.slice_in_dim(cells, cells.shape[dim] - width, cells.shape[dim], axis=dim)
        cells = jnp.concatenate(
            [
                lax.ppermute(tail, axis, [(i, (i + 1) % count) for i in range(count)]),
                cells,
                lax.ppermute(head, axis, [((i + 1) % count, i) for i in range(count)]),
            ],
            axis=dim,
        )
    return cells


def band_matrix(weights, sources, targets, shift, period):
    source_idx = lax.broadcasted_iota(jnp.int32, (sources, targets), 0)
    target_idx = lax.broadcasted_iota(jnp.int32, (sources, targets), 1)
    offset = source_idx - target_idx + shift
    if period > 0:
        offset = offset % period
    tap_index = jnp.arange(weights.shape[0], dtype=jnp.int32)
    one_hot = (offset[:, :, None] == tap_index[None, None, :]).astype(jnp.float32)
    return jnp.einsum("abt,t->ab", one_hot, weights, precision=HIGHEST)


def contract(values, along, matrix):
    result = jnp.tensordot(values, matrix, axes=((along,), (0,)), precision=HIGHEST)
    return jnp.moveaxis(result, -1, along)


def dft_table(period, sources, targets):
    product = sources[:, None] * targets[None, :] % period
    phases = 2.0 * math.pi / period * product.astype(jnp.float32)
    return (jnp.cos(phases), jnp.sin(phases))


def transform(spectrum, along, table, orient):
    cosine, sine_part = table
    real_part = contract(spectrum[0], along, cosine) - orient * contract(
        spectrum[1], along, sine_part
    )
    imag_part = contract(spectrum[1], along, cosine) + orient * contract(
        spectrum[0], along, sine_part
    )
    return jnp.stack([real_part, imag_part])


def spectral(spectrum, wave_x, wave_y, wave_z, count_x, count_y, count_z):
    phase_x = 2.0 * math.pi / count_x * wave_x.astype(jnp.float32)
    phase_y = 2.0 * math.pi / count_y * wave_y.astype(jnp.float32)
    phase_z = 2.0 * math.pi / count_z * wave_z.astype(jnp.float32)
    laplace = (
        (2.0 - 2.0 * jnp.cos(phase_x))[:, None, None]
        + (2.0 - 2.0 * jnp.cos(phase_y))[None, :, None]
        + (2.0 - 2.0 * jnp.cos(phase_z))[None, None, :]
    )
    anchor = (
        (wave_x[:, None, None] == 0) & (wave_y[None, :, None] == 0) & (wave_z[None, None, :] == 0)
    )
    weight_k = jnp.where(anchor, 0.0, 1.0 / jnp.where(anchor, 1.0, laplace)) / float(
        count_x * count_y * count_z
    )
    sine_list = [
        jnp.sin(phase_x)[:, None, None],
        jnp.sin(phase_y)[None, :, None],
        jnp.sin(phase_z)[None, None, :],
    ]
    real_part = jnp.stack([-sine_part * spectrum[1] * weight_k for sine_part in sine_list])
    imag_part = jnp.stack([sine_part * spectrum[0] * weight_k for sine_part in sine_list])
    return jnp.stack([real_part, imag_part])


def short_forces(density, smooth_taps, deriv_taps):
    radius = (smooth_taps.shape[0] - 1) // 2
    padded = extended(density, (("gx", 0), ("gy", 1)), radius)
    rows_in = padded.shape[0]
    smooth_rows = band_matrix(smooth_taps, rows_in, rows_in - 2 * radius, 0, 0)
    deriv_rows = band_matrix(deriv_taps, rows_in, rows_in - 2 * radius, 0, 0)
    smooth_x = jnp.einsum("jyz,ji->iyz", padded, smooth_rows, precision=HIGHEST)
    deriv_x = jnp.einsum("jyz,ji->iyz", padded, deriv_rows, precision=HIGHEST)
    cols_in = smooth_x.shape[1]
    smooth_cols = band_matrix(smooth_taps, cols_in, cols_in - 2 * radius, 0, 0)
    deriv_cols = band_matrix(deriv_taps, cols_in, cols_in - 2 * radius, 0, 0)
    depth = density.shape[2]
    smooth_depth = band_matrix(smooth_taps, depth, depth, radius, depth)
    deriv_depth = band_matrix(deriv_taps, depth, depth, radius, depth)
    first = jnp.einsum("xjz,ji->xiz", deriv_x, smooth_cols, precision=HIGHEST)
    second = jnp.einsum("xjz,ji->xiz", smooth_x, deriv_cols, precision=HIGHEST)
    third = jnp.einsum("xjz,ji->xiz", smooth_x, smooth_cols, precision=HIGHEST)
    return jnp.stack(
        [
            jnp.einsum("xyj,ji->xyi", first, smooth_depth, precision=HIGHEST),
            jnp.einsum("xyj,ji->xyi", second, smooth_depth, precision=HIGHEST),
            jnp.einsum("xyj,ji->xyi", third, deriv_depth, precision=HIGHEST),
        ]
    )


def long_forces(density):
    tile_x = density.shape[0] // FACTOR
    tile_y = density.shape[1] // FACTOR
    tile_z = density.shape[2] // FACTOR
    coarse = density.reshape(tile_x, FACTOR, tile_y, FACTOR, tile_z, FACTOR).mean(axis=(1, 3, 5))
    count_x = tile_x * lax.axis_size("gx")
    count_y = tile_y * lax.axis_size("gy")
    depth_all = jnp.arange(tile_z, dtype=jnp.int32)
    depth_table = dft_table(tile_z, depth_all, depth_all)
    spectrum = jnp.stack(
        [contract(coarse, 2, depth_table[0]), -contract(coarse, 2, depth_table[1])]
    )
    cols_all = jnp.arange(count_y, dtype=jnp.int32)
    cols_table = dft_table(count_y, cols_all, cols_all)
    spectrum = lax.all_gather(spectrum, "gy", axis=2, tiled=True)
    spectrum = transform(spectrum, 1, cols_table, -1.0)
    spectrum = lax.all_to_all(spectrum, "gx", split_axis=2, concat_axis=1, tiled=True)
    rows_all = jnp.arange(count_x, dtype=jnp.int32)
    rows_table = dft_table(count_x, rows_all, rows_all)
    spectrum = transform(spectrum, 0, rows_table, -1.0)
    wave_y = lax.axis_index("gx") * spectrum.shape[2] + jnp.arange(
        spectrum.shape[2], dtype=jnp.int32
    )
    wave_z = jnp.arange(spectrum.shape[3], dtype=jnp.int32)
    fields = spectral(spectrum, rows_all, wave_y, wave_z, count_x, count_y, tile_z)
    fields = transform(fields, 1, rows_table, 1.0)
    fields = lax.all_to_all(fields, "gx", split_axis=2, concat_axis=3, tiled=True)
    mine = lax.axis_index("gy") * tile_y + jnp.arange(tile_y, dtype=jnp.int32)
    fields = transform(fields, 2, dft_table(count_y, cols_all, mine), 1.0)
    return contract(fields[0], 3, depth_table[0]) - contract(fields[1], 3, depth_table[1])


def per_device(density, momenta, smooth_taps, deriv_taps, kick_step):
    long_range = long_forces(density)
    short_range = short_forces(density, smooth_taps, deriv_taps)
    fine_long = jnp.repeat(jnp.repeat(jnp.repeat(long_range, FACTOR, 1), FACTOR, 2), FACTOR, 3)
    forces = short_range + LONG_COUPLING * fine_long
    return momenta + kick_step * forces


def solution(mesh):
    in_specs = (P("gx", "gy", None), P(None, "gx", "gy", None), P(), P(), P())
    out_specs = P(None, "gx", "gy", None)
    return jax.shard_map(
        per_device, mesh=mesh, in_specs=in_specs, out_specs=out_specs, check_vma=False
    )
```

profile of v0, /device:TPU:0, one launch (start us, length us, event | category | flops | bytes accessed | tf_op | source)
XLA Modules:
  0.0 103.8 jit_solution(2877908469738453902)
XLA Ops:
  0.0 1.1 %copy.173 = f32[16,48,128]{2,0,1:T(8,128)S(1)} copy(f32[16,48,128]{2,1,0:T(8,128)} %param.5) | data formatting | bytes 786432 | tf_op args[0]
  1.1 0.5 collective-permute-start
  1.7 4.1 %collective-permute-start.1 = (f32[16,48,128]{2,0,1:T(8,128)S(1)}, f32[16,48,128]{2,0,1:T(8,128)S(1)}, u32[]{:S(2)}, u32[]{:S(2)}) collective-permute-start(f32[16,48,128]{2,0,1:T(8,128)S(1)} %copy.173), channel_id=1, source_target_pairs={{4,0},{8,4},{12,8},{16,12},{20,16},{24,20},{28,24},{0,28},{5,1},{9... | collective-permute-start | bytes 1179656 | tf_op jit(solution)/shard_map/ppermute | solution.py:21
  5.8 15.2 %reshape.181 = f32[4,4,12,4,32,4]{5,4,3,2,1,0:T(8,128)} reshape(f32[16,48,128]{2,1,0:T(8,128)} %param.5) | data formatting | bytes 786432 | tf_op jit(solution)/shard_map/reshape | solution.py:116
  20.9 5.6 %reduce_sum.9 = f32[4,12,32]{2,1,0:T(8,128)S(1)} reduce(f32[4,4,12,4,32,4]{5,4,3,2,1,0:T(8,128)} %reshape.181, f32[]{:T(128)} %constant.82.clone.1), dimensions={1,3,5}, to_apply=%region_0.0 | reduce | flops 96768 | bytes 399364 | tf_op jit(solution)/shard_map/reduce_sum | solution.py:116
  26.5 0.2 convolution_bitcast_fusion.6
  26.7 0.2 fusion.19
  27.0 9.3 %all_gather.3 = f32[2,4,48,32]{3,1,0,2:T(4,128)S(1)} all-gather(f32[2,4,12,32]{3,1,0,2:T(4,128)S(1)} %copy.179), channel_id=1, replica_groups=mesh['gx'=8,'gy'=4] {'gy'}, dimensions={2}, use_global_device_ids=true | all-gather | bytes 61440 | tf_op jit(solution)/shard_map/all_gather | solution.py:126
  36.5 0.3 fusion.35
  36.9 0.3 fusion.31
  37.2 0.3 fusion.18
  37.5 0.3 fusion.16
  37.9 0.1 copy.182
  38.0 0.8 reshape.212
  38.8 3.5 %all-to-all-start = ((f32[8,1,1536]{2,1,0:T(1,128)}), f32[8,1,1536]{2,1,0:T(1,128)S(1)}, u32[]{:S(2)}, u32[]{:S(2)}) async-start(f32[8,1,1536]{2,1,0:T(1,128)} %reshape.212), calls=%async_computation | async-start | bytes 98304 | tf_op jit(solution)/shard_map/all_to_all | solution.py:128
  42.7 0.9 fusion.24
  43.7 0.9 fusion.23
  44.6 1.0 select_reduce_fusion.1
  45.6 0.3 iota_compare_fusion
  45.9 1.9 %fusion = f32[1,128,128]{2,0,1:T(1,128)} fusion(pred[128,128,33]{1,0,2:T(32,128)(4,1)S(1)} %iota_compare_fusion, f32[33]{0:T(128)S(1)} %copy-done.10), kind=kOutput, calls=%fused_computation | convolution fusion | flops 6488064 | bytes 606340 | tf_op jit(solution)/shard_map/abt,t->ab/dot_general | solution.py:36
  48.1 0.5 broadcast.337
  48.6 0.7 reduce.4
  49.3 0.1 reshape.213
  49.5 0.4 fusion.69
  49.9 0.4 fusion.72
  50.3 0.4 fusion.13
  50.6 0.4 multiply_bitcast_fusion.5
  51.0 0.6 fusion.27
  51.7 0.6 fusion.26
  52.3 0.6 fusion.9
  53.0 0.6 fusion.8
  53.7 0.3 copy.194
  54.1 1.3 %reshape.214 = f32[8,1,4608]{2,1,0:T(1,128)} reshape(f32[32,3,6,2,32]{4,3,2,1,0:T(2,128)S(1)} %bitcast.198) | data formatting | bytes 294912
  55.3 4.8 %all-to-all-start.1 = ((f32[8,1,4608]{2,1,0:T(1,128)}), f32[8,1,4608]{2,1,0:T(1,128)S(1)}, u32[]{:S(2)}, u32[]{:S(2)}) async-start(f32[8,1,4608]{2,1,0:T(1,128)} %reshape.214), calls=%async_computation.1 | async-start | bytes 294912 | tf_op jit(solution)/shard_map/all_to_all | solution.py:138
  60.8 1.9 %fusion.2 = f32[1,128,128]{2,0,1:T(1,128)} fusion(pred[128,128,33]{1,0,2:T(32,128)(4,1)S(1)} %iota_compare_fusion, f32[33]{0:T(128)S(1)} %copy-done.11), kind=kOutput, calls=%fused_computation.2 | convolution fusion | flops 6488064 | bytes 606340 | tf_op jit(solution)/shard_map/abt,t->ab/dot_general | solution.py:36
  62.8 4.4 %all-to-all-done.1 = f32[8,1,4608]{2,1,0:T(1,128)S(1)} async-done(((f32[8,1,4608]{2,1,0:T(1,128)}), f32[8,1,4608]{2,1,0:T(1,128)S(1)}, u32[]{:S(2)}, u32[]{:S(2)}) %all-to-all-start.1) | async-done | bytes 147488 | tf_op jit(solution)/shard_map/all_to_all | solution.py:138
  67.1 0.9 reduce.5
  68.0 0.5 reshape.215
  68.7 0.1 copy.199
  68.9 0.1 copy.197
  69.1 0.9 fusion.95
  70.0 1.0 fusion.11
  71.0 1.0 fusion.97
  71.9 1.0 fusion.12
  73.1 1.0 fusion.227
  74.1 1.4 %collective-permute-start.2 = (f32[48,16,128]{2,0,1:T(8,128)}, f32[48,16,128]{2,0,1:T(8,128)S(1)}, u32[]{:S(2)}, u32[]{:S(2)}) collective-permute-start(f32[48,16,128]{2,0,1:T(8,128)} %get-tuple-element.7), channel_id=1, source_target_pairs={{0,1},{1,2},{2,3},{3,0},{4,5},{5,6},{6,7},{7,4},{8,9},{9,10},{10,1... | collective-permute-start | bytes 1179656 | tf_op jit(solution)/shard_map/ppermute | solution.py:19
  75.5 1.6 %collective-permute-start.3 = (f32[48,16,128]{2,0,1:T(8,128)}, f32[48,16,128]{2,0,1:T(8,128)}, u32[]{:S(2)}, u32[]{:S(2)}) collective-permute-start(f32[48,16,128]{2,0,1:T(8,128)} %get-tuple-element.8), channel_id=1, source_target_pairs={{1,0},{2,1},{3,2},{0,3},{5,4},{6,5},{7,6},{4,7},{9,8},{10,9},{11,1... | collective-permute-start | bytes 1179656 | tf_op jit(solution)/shard_map/ppermute | solution.py:21
  77.1 0.3 fusion.62
  77.4 0.3 fusion.10
  77.9 1.5 %copy.203 = f32[3,16,48,32]{2,1,3,0:T(8,128)} copy(f32[3,16,48,32]{3,1,2,0:T(8,128)S(1)} %bitcast.196) | data formatting | bytes 589824 | tf_op jit(solution)/shard_map/mul | solution.py:148
  79.4 1.4 %broadcast_in_dim.14 = f32[3,16,48,32,4]{2,1,4,3,0:T(8,128)S(1)} broadcast(f32[3,16,48,32]{2,1,3,0:T(8,128)} %copy.203), dimensions={0,1,2,3} | broadcast | bytes 1474560 | tf_op jit(solution)/shard_map/broadcast_in_dim | solution.py:147
  80.8 1.9 %copy.204 = f32[3,16,48,128]{3,2,1,0:T(8,128)} copy(f32[3,16,48,128]{2,1,3,0:T(8,128)S(1)} %bitcast.195) | data formatting | bytes 2359296 | tf_op jit(solution)/shard_map/mul | solution.py:148
  82.7 4.5 %collective-permute-done.2 = f32[48,16,128]{2,0,1:T(8,128)S(1)} collective-permute-done((f32[48,16,128]{2,0,1:T(8,128)}, f32[48,16,128]{2,0,1:T(8,128)S(1)}, u32[]{:S(2)}, u32[]{:S(2)}) %collective-permute-start.2) | collective-permute-done | bytes 393248 | tf_op jit(solution)/shard_map/ppermute | solution.py:19
  87.2 7.0 %collective-permute-done.3 = f32[48,16,128]{2,0,1:T(8,128)} collective-permute-done((f32[48,16,128]{2,0,1:T(8,128)}, f32[48,16,128]{2,0,1:T(8,128)}, u32[]{:S(2)}, u32[]{:S(2)}) %collective-permute-start.3) | collective-permute-done | bytes 393248 | tf_op jit(solution)/shard_map/ppermute | solution.py:21
  94.2 2.5 %fusion.4 = f32[16,80,128]{2,0,1:T(8,128)S(1)} fusion(f32[48,16,128]{2,0,1:T(8,128)} %collective-permute-done.3, f32[48,48,128]{2,0,1:T(8,128)} %copy-done, f32[48,16,128]{2,0,1:T(8,128)S(1)} %collective-permute-done.2, f32[48,16]{1,0:T(8,128)} %get-tuple-element.6), kind=kOutput, calls=%fused_computation.6 | convolution fusion | flops 95354880 | bytes 2624512 | tf_op jit(solution)/shard_map/jyz,ji->iyz/dot_general | solution.py:92
  96.7 0.7 convolution_bitcast_fusion.1
  97.4 0.7 convolution_bitcast_fusion.3
  98.1 2.1 %fusion.5 = f32[16,80,128]{2,0,1:T(8,128)S(1)} fusion(f32[48,16,128]{2,0,1:T(8,128)} %collective-permute-done.3, f32[48,48,128]{2,0,1:T(8,128)S(1)} %copy-done.1, f32[48,16,128]{2,0,1:T(8,128)S(1)} %collective-permute-done.2, f32[48,16]{1,0:T(8,128)S(1)} %copy-done.6), kind=kOutput, calls=%fused_computation.7 | convolution fusion | flops 95354880 | bytes 2624512 | tf_op jit(solution)/shard_map/jyz,ji->iyz/dot_general | solution.py:93
  100.2 0.7 convolution_bitcast_fusion.5
  101.0 0.5 convolution_bitcast_fusion.2
  101.4 0.5 convolution_bitcast_fusion.4
  101.9 0.5 convolution_bitcast_fusion
  102.4 0.2 copy-done.4
  102.6 1.2 %fusion.7 = f32[3,16,48,128]{3,2,1,0:T(8,128)} fusion(f32[3,16,48,128]{3,2,1,0:T(8,128)S(1)} %copy-done.4, f32[3,16,48,128]{3,2,1,0:T(8,128)S(1)} %copy-done.2, f32[1,16,48,128]{3,2,1,0:T(8,128)S(1)} %convolution_bitcast_fusion, f32[1,16,48,128]{3,2,1,0:T(8,128)S(1)} %convolution_bitcast_fusion.2, f32[1,16,48,128]{3,2,1,0:T(8,128)S(1)} %convolution_bitcast_fusion.4, ...), kind=kLoop, calls=%fused_computation.16 | loop fusion | flops 1474560 | bytes 4718596 | tf_op jit(solution)/shard_map/add | solution.py:149
  (60 shorter events, 1.5 us)
Async XLA Ops:
  1.1 71.8 %collective-permute-start = (f32[16,48,128]{2,0,1:T(8,128)S(1)}, f32[16,48,128]{2,0,1:T(8,128)S(1)}, u32[]{:S(2)}, u32[]{:S(2)}) collective-permute-start(f32[16,48,128]{2,0,1:T(8,128)S(1)} %copy.173), channel_id=1, source_target_pairs={{0,4},{4,8},{8,12},{12,16},{16,20},{20,24},{24,28},{28,0},{1,5},{5... | collective-permute-start | bytes 1179656 | tf_op jit(solution)/shard_map/ppermute | solution.py:19
  1.7 71.4 %collective-permute-start.1 = (f32[16,48,128]{2,0,1:T(8,128)S(1)}, f32[16,48,128]{2,0,1:T(8,128)S(1)}, u32[]{:S(2)}, u32[]{:S(2)}) collective-permute-start(f32[16,48,128]{2,0,1:T(8,128)S(1)} %copy.173), channel_id=1, source_target_pairs={{4,0},{8,4},{12,8},{16,12},{20,16},{24,20},{28,24},{0,28},{5,1},{9... | collective-permute-start | bytes 1179656 | tf_op jit(solution)/shard_map/ppermute | solution.py:21
  36.4 6.3 %copy-start.11 = (f32[33]{0:T(128)S(1)}, f32[33]{0:T(128)}, u32[]{:S(2)}) copy-start(f32[33]{0:T(128)} %param.7) | copy-start | bytes 400
  37.2 6.5 %copy-start.10 = (f32[33]{0:T(128)S(1)}, f32[33]{0:T(128)}, u32[]{:S(2)}) copy-start(f32[33]{0:T(128)} %param.8) | copy-start | bytes 400
  38.8 9.2 %all-to-all-start = ((f32[8,1,1536]{2,1,0:T(1,128)}), f32[8,1,1536]{2,1,0:T(1,128)S(1)}, u32[]{:S(2)}, u32[]{:S(2)}) async-start(f32[8,1,1536]{2,1,0:T(1,128)} %reshape.212), calls=%async_computation | async-start | bytes 98304 | tf_op jit(solution)/shard_map/all_to_all | solution.py:128
  55.3 11.8 %all-to-all-start.1 = ((f32[8,1,4608]{2,1,0:T(1,128)}), f32[8,1,4608]{2,1,0:T(1,128)S(1)}, u32[]{:S(2)}, u32[]{:S(2)}) async-start(f32[8,1,4608]{2,1,0:T(1,128)} %reshape.214), calls=%async_computation.1 | async-start | bytes 294912 | tf_op jit(solution)/shard_map/all_to_all | solution.py:138
  69.1 3.9 %copy-start.3 = (f32[16,48,128]{2,1,0:T(8,128)S(1)}, f32[16,48,128]{2,1,0:T(8,128)}, u32[]{:S(2)}) copy-start(f32[16,48,128]{2,1,0:T(8,128)} %param.5) | copy-start | bytes 1179652
  73.1 4.7 %copy-start = (f32[48,48,128]{2,0,1:T(8,128)}, f32[48,48,128]{2,0,1:T(8,128)S(1)}, u32[]{:S(2)}) copy-start(f32[48,48,128]{2,0,1:T(8,128)S(1)} %constant_dynamic-update-slice_fusion) | copy-start | bytes 3538948
  74.1 13.1 %collective-permute-start.2 = (f32[48,16,128]{2,0,1:T(8,128)}, f32[48,16,128]{2,0,1:T(8,128)S(1)}, u32[]{:S(2)}, u32[]{:S(2)}) collective-permute-start(f32[48,16,128]{2,0,1:T(8,128)} %get-tuple-element.7), channel_id=1, source_target_pairs={{0,1},{1,2},{2,3},{3,0},{4,5},{5,6},{6,7},{7,4},{8,9},{9,10},{10,1... | collective-permute-start | bytes 1179656 | tf_op jit(solution)/shard_map/ppermute | solution.py:19
  75.5 18.7 %collective-permute-start.3 = (f32[48,16,128]{2,0,1:T(8,128)}, f32[48,16,128]{2,0,1:T(8,128)}, u32[]{:S(2)}, u32[]{:S(2)}) collective-permute-start(f32[48,16,128]{2,0,1:T(8,128)} %get-tuple-element.8), channel_id=1, source_target_pairs={{1,0},{2,1},{3,2},{0,3},{5,4},{6,5},{7,6},{4,7},{9,8},{10,9},{11,1... | collective-permute-start | bytes 1179656 | tf_op jit(solution)/shard_map/ppermute | solution.py:21
  94.2 2.5 %copy-start.7 = (f32[1,80,48]{1,0,2:T(1,128)S(1)}, f32[1,80,48]{1,0,2:T(1,128)}, u32[]{:S(2)}) copy-start(f32[1,80,48]{1,0,2:T(1,128)} %fusion.24) | copy-start | bytes 46084
  94.2 3.2 %copy-start.9 = (f32[1,80,48]{1,0,2:T(1,128)S(1)}, f32[1,80,48]{1,0,2:T(1,128)}, u32[]{:S(2)}) copy-start(f32[1,80,48]{1,0,2:T(1,128)} %fusion.23) | copy-start | bytes 46084
  96.7 1.4 %copy-start.1 = (f32[48,48,128]{2,0,1:T(8,128)S(1)}, f32[48,48,128]{2,0,1:T(8,128)}, u32[]{:S(2)}) copy-start(f32[48,48,128]{2,0,1:T(8,128)} %copy-done) | copy-start | bytes 3538948
  96.7 1.4 %copy-start.6 = (f32[48,16]{1,0:T(8,128)S(1)}, f32[48,16]{1,0:T(8,128)}, u32[]{:S(2)}) copy-start(f32[48,16]{1,0:T(8,128)} %get-tuple-element.5) | copy-start | bytes 9220
  98.1 2.8 %copy-start.5 = (f32[1,128,128]{2,0,1:T(1,128)S(1)}, f32[1,128,128]{2,0,1:T(1,128)}, u32[]{:S(2)}) copy-start(f32[1,128,128]{2,0,1:T(1,128)} %fusion.2) | copy-start | bytes 196612
  100.2 1.7 %copy-start.8 = (f32[1,128,128]{2,0,1:T(1,128)S(1)}, f32[1,128,128]{2,0,1:T(1,128)}, u32[]{:S(2)}) copy-start(f32[1,128,128]{2,0,1:T(1,128)} %fusion) | copy-start | bytes 196612
  100.9 1.4 %copy-start.2 = (f32[3,16,48,128]{3,2,1,0:T(8,128)S(1)}, f32[3,16,48,128]{3,2,1,0:T(8,128)}, u32[]{:S(2)}) copy-start(f32[3,16,48,128]{3,2,1,0:T(8,128)} %copy.204) | copy-start | bytes 3538948
  100.9 1.6 %copy-start.4 = (f32[3,16,48,128]{3,2,1,0:T(8,128)S(1)}, f32[3,16,48,128]{3,2,1,0:T(8,128)}, u32[]{:S(2)}) copy-start(f32[3,16,48,128]{3,2,1,0:T(8,128)} %param.6) | copy-start | bytes 3538948
where the time goes:
time: 104 us
  local copies, waits for them, and re-layouts  27.2 us (26%)
  matrix products  24 us (23%)
  starting transfers between devices  15.9 us (15%)
  waiting for transfers between devices  15.8 us (15%)
  other arithmetic  10.2 us (10%)
  blocking collectives  9.29 us (9%)
  between operations  1.3 us (1%)
    reshape x1, local copies, waits for them, and re-layouts, long_forces(): density.reshape(tile_x, FACTOR, tile_y, FACTOR, tile_z, FACTOR)  15.2 us
    dot_general x20, matrix products, contract(): jnp.tensordot(values, matrix, axes=((along,), (0,)), precision=HIGHEST)  10.2 us
    all_gather x1, blocking collectives, long_forces(): spectrum = lax.all_gather(spectrum, 'gy', axis=2, tiled=True)  9.29 us
    ppermute x2, waiting for transfers between devices, extended(): lax.ppermute(head, axis, [((i + 1) % count, i) for i in range(count)])  6.97 us
    dot_general x4, matrix products, band_matrix(): return jnp.einsum('abt,t->ab', one_hot, weights, precision=HIGHEST)  5.77 us
    ppermute x2, starting transfers between devices, extended(): lax.ppermute(head, axis, [((i + 1) % count, i) for i in range(count)])  5.65 us
    reduce_sum x1, other arithmetic, long_forces(): density.reshape(tile_x, FACTOR, tile_y, FACTOR, tile_z, FACTOR)  5.57 us
    all_to_all x1, starting transfers between devices, long_forces(): lax.all_to_all(fields, 'gx', split_axis=2, concat_axis=3, tiled=True)  4.85 us
  transfers between devices with their start and end apart: 6, of which 3 were waited for; matrix products, arithmetic and copies ran while one was open for 48% of the time, Pallas kernels for 0%

commit v1 on v0

--- a/solution.py
+++ b/solution.py
@@ -123,7 +123,7 @@
     )
     cols_all = jnp.arange(count_y, dtype=jnp.int32)
     cols_table = dft_table(count_y, cols_all, cols_all)
-    spectrum = lax.all_gather(spectrum, "gy", axis=2, tiled=True)
+    spectrum = jnp.concatenate(lax.all_gather(spectrum, "gy"), axis=2)
     spectrum = transform(spectrum, 1, cols_table, -1.0)
     spectrum = lax.all_to_all(spectrum, "gx", split_axis=2, concat_axis=1, tiled=True)
     rows_all = jnp.arange(count_x, dtype=jnp.int32)

time: 104 us -> 104 us (level)
    unnamed x33 -> x31, local copies, waits for them, and re-layouts: 4.37 us -> 4.21 us
where the time goes in v1:
time: 104 us
  local copies, waits for them, and re-layouts  27.2 us (26%)
  matrix products  24 us (23%)
  starting transfers between devices  15.9 us (15%)
  waiting for transfers between devices  15.8 us (15%)
  other arithmetic  10.2 us (10%)
  blocking collectives  9.29 us (9%)
  between operations  1.31 us (1%)
    reshape x1, local copies, waits for them, and re-layouts, long_forces(): density.reshape(tile_x, FACTOR, tile_y, FACTOR, tile_z, FACTOR)  15.2 us
    dot_general x20, matrix products, contract(): jnp.tensordot(values, matrix, axes=((along,), (0,)), precision=HIGHEST)  10.2 us
    all_gather x1, blocking collectives, long_forces(): spectrum = jnp.concatenate(lax.all_gather(spectrum, 'gy'), axis=2)  9.29 us
    ppermute x2, waiting for transfers between devices, extended(): lax.ppermute(head, axis, [((i + 1) % count, i) for i in range(count)])  6.97 us
    dot_general x4, matrix products, band_matrix(): return jnp.einsum('abt,t->ab', one_hot, weights, precision=HIGHEST)  5.77 us
    ppermute x2, starting transfers between devices, extended(): lax.ppermute(head, axis, [((i + 1) % count, i) for i in range(count)])  5.65 us
    reduce_sum x1, other arithmetic, long_forces(): density.reshape(tile_x, FACTOR, tile_y, FACTOR, tile_z, FACTOR)  5.57 us
    all_to_all x1, starting transfers between devices, long_forces(): lax.all_to_all(fields, 'gx', split_axis=2, concat_axis=3, tiled=True)  4.84 us
  transfers between devices with their start and end apart: 6, of which 3 were waited for; matrix products, arithmetic and copies ran while one was open for 48% of the time, Pallas kernels for 0%

profile of v1, /device:TPU:0, one launch (start us, length us, event | category | flops | bytes accessed | tf_op | source)
XLA Modules:
  0.0 103.8 jit_solution(3766774510523758043)
XLA Ops:
  0.0 1.1 %copy.182 = f32[16,48,128]{2,0,1:T(8,128)S(1)} copy(f32[16,48,128]{2,1,0:T(8,128)} %param.5) | data formatting | bytes 786432 | tf_op args[0]
  1.1 0.5 collective-permute-start
  1.7 4.1 %collective-permute-start.1 = (f32[16,48,128]{2,0,1:T(8,128)S(1)}, f32[16,48,128]{2,0,1:T(8,128)S(1)}, u32[]{:S(2)}, u32[]{:S(2)}) collective-permute-start(f32[16,48,128]{2,0,1:T(8,128)S(1)} %copy.182), channel_id=1, source_target_pairs={{4,0},{8,4},{12,8},{16,12},{20,16},{24,20},{28,24},{0,28},{5,1},{9... | collective-permute-start | bytes 1179656 | tf_op jit(solution)/shard_map/ppermute | solution.py:21
  5.8 15.2 %reshape.189 = f32[4,4,12,4,32,4]{5,4,3,2,1,0:T(8,128)} reshape(f32[16,48,128]{2,1,0:T(8,128)} %param.5) | data formatting | bytes 786432 | tf_op jit(solution)/shard_map/reshape | solution.py:116
  20.9 5.6 %reduce_sum.9 = f32[4,12,32]{2,1,0:T(8,128)S(1)} reduce(f32[4,4,12,4,32,4]{5,4,3,2,1,0:T(8,128)} %reshape.189, f32[]{:T(128)} %constant.82.clone.1), dimensions={1,3,5}, to_apply=%region_0.0 | reduce | flops 96768 | bytes 399364 | tf_op jit(solution)/shard_map/reduce_sum | solution.py:116
  26.5 0.2 convolution_bitcast_fusion.6
  26.7 0.2 fusion.19
  27.0 9.3 %all-gather = f32[8,4,12,32]{3,1,2,0:T(4,128)S(1)} all-gather(f32[2,4,12,32]{3,1,2,0:T(4,128)S(1)} %copy.188), channel_id=2, replica_groups=mesh['gx'=8,'gy'=4] {'gy'}, dimensions={0}, use_global_device_ids=true | all-gather | bytes 61440 | tf_op jit(solution)/shard_map/all_gather | solution.py:126
  36.5 0.3 fusion.39
  36.9 0.3 fusion.37
  37.2 0.3 fusion.18
  37.5 0.3 fusion.16
  37.9 0.1 copy.194
  38.0 0.8 reshape.222
  38.8 3.5 %all-to-all-start = ((f32[8,1,1536]{2,1,0:T(1,128)}), f32[8,1,1536]{2,1,0:T(1,128)S(1)}, u32[]{:S(2)}, u32[]{:S(2)}) async-start(f32[8,1,1536]{2,1,0:T(1,128)} %reshape.222), calls=%async_computation | async-start | bytes 98304 | tf_op jit(solution)/shard_map/all_to_all | solution.py:128
  42.7 0.9 fusion.24
  43.7 0.9 fusion.23
  44.6 1.0 select_reduce_fusion.1
  45.6 0.3 iota_compare_fusion
  45.9 1.9 %fusion = f32[1,128,128]{2,0,1:T(1,128)} fusion(pred[128,128,33]{1,0,2:T(32,128)(4,1)S(1)} %iota_compare_fusion, f32[33]{0:T(128)S(1)} %copy-done.10), kind=kOutput, calls=%fused_computation | convolution fusion | flops 6488064 | bytes 606340 | tf_op jit(solution)/shard_map/abt,t->ab/dot_general | solution.py:36
  48.1 0.5 broadcast.337
  48.6 0.7 reduce.4
  49.3 0.1 reshape.223
  49.5 0.4 fusion.65
  49.9 0.4 fusion.68
  50.3 0.4 fusion.13
  50.7 0.4 multiply_bitcast_fusion.5
  51.1 0.6 fusion.27
  51.7 0.6 fusion.26
  52.4 0.6 fusion.9
  53.0 0.6 fusion.8
  53.7 0.3 copy.206
  54.1 1.3 %reshape.224 = f32[8,1,4608]{2,1,0:T(1,128)} reshape(f32[32,3,6,2,32]{4,3,2,1,0:T(2,128)S(1)} %bitcast.198) | data formatting | bytes 294912
  55.3 4.8 %all-to-all-start.1 = ((f32[8,1,4608]{2,1,0:T(1,128)}), f32[8,1,4608]{2,1,0:T(1,128)S(1)}, u32[]{:S(2)}, u32[]{:S(2)}) async-start(f32[8,1,4608]{2,1,0:T(1,128)} %reshape.224), calls=%async_computation.1 | async-start | bytes 294912 | tf_op jit(solution)/shard_map/all_to_all | solution.py:138
  60.8 1.9 %fusion.2 = f32[1,128,128]{2,0,1:T(1,128)} fusion(pred[128,128,33]{1,0,2:T(32,128)(4,1)S(1)} %iota_compare_fusion, f32[33]{0:T(128)S(1)} %copy-done.11), kind=kOutput, calls=%fused_computation.2 | convolution fusion | flops 6488064 | bytes 606340 | tf_op jit(solution)/shard_map/abt,t->ab/dot_general | solution.py:36
  62.8 4.4 %all-to-all-done.1 = f32[8,1,4608]{2,1,0:T(1,128)S(1)} async-done(((f32[8,1,4608]{2,1,0:T(1,128)}), f32[8,1,4608]{2,1,0:T(1,128)S(1)}, u32[]{:S(2)}, u32[]{:S(2)}) %all-to-all-start.1) | async-done | bytes 147488 | tf_op jit(solution)/shard_map/all_to_all | solution.py:138
  67.1 0.9 reduce.5
  68.0 0.5 reshape.225
  68.7 0.1 copy.211
  68.9 0.1 copy.209
  69.1 0.9 fusion.91
  70.0 1.0 fusion.11
  71.0 1.0 fusion.93
  71.9 1.0 fusion.12
  73.2 1.0 fusion.223
  74.1 1.4 %collective-permute-start.2 = (f32[48,16,128]{2,0,1:T(8,128)}, f32[48,16,128]{2,0,1:T(8,128)S(1)}, u32[]{:S(2)}, u32[]{:S(2)}) collective-permute-start(f32[48,16,128]{2,0,1:T(8,128)} %get-tuple-element.7), channel_id=1, source_target_pairs={{0,1},{1,2},{2,3},{3,0},{4,5},{5,6},{6,7},{7,4},{8,9},{9,10},{10,1... | collective-permute-start | bytes 1179656 | tf_op jit(solution)/shard_map/ppermute | solution.py:19
  75.5 1.6 %collective-permute-start.3 = (f32[48,16,128]{2,0,1:T(8,128)}, f32[48,16,128]{2,0,1:T(8,128)}, u32[]{:S(2)}, u32[]{:S(2)}) collective-permute-start(f32[48,16,128]{2,0,1:T(8,128)} %get-tuple-element.8), channel_id=1, source_target_pairs={{1,0},{2,1},{3,2},{0,3},{5,4},{6,5},{7,6},{4,7},{9,8},{10,9},{11,1... | collective-permute-start | bytes 1179656 | tf_op jit(solution)/shard_map/ppermute | solution.py:21
  77.1 0.3 fusion.58
  77.4 0.3 fusion.10
  77.9 1.5 %copy.215 = f32[3,16,48,32]{2,1,3,0:T(8,128)} copy(f32[3,16,48,32]{3,1,2,0:T(8,128)S(1)} %bitcast.196) | data formatting | bytes 589824 | tf_op jit(solution)/shard_map/mul | solution.py:148
  79.4 1.4 %broadcast_in_dim.14 = f32[3,16,48,32,4]{2,1,4,3,0:T(8,128)S(1)} broadcast(f32[3,16,48,32]{2,1,3,0:T(8,128)} %copy.215), dimensions={0,1,2,3} | broadcast | bytes 1474560 | tf_op jit(solution)/shard_map/broadcast_in_dim | solution.py:147
  80.8 1.9 %copy.216 = f32[3,16,48,128]{3,2,1,0:T(8,128)} copy(f32[3,16,48,128]{2,1,3,0:T(8,128)S(1)} %bitcast.195) | data formatting | bytes 2359296 | tf_op jit(solution)/shard_map/mul | solution.py:148
  82.7 4.5 %collective-permute-done.2 = f32[48,16,128]{2,0,1:T(8,128)S(1)} collective-permute-done((f32[48,16,128]{2,0,1:T(8,128)}, f32[48,16,128]{2,0,1:T(8,128)S(1)}, u32[]{:S(2)}, u32[]{:S(2)}) %collective-permute-start.2) | collective-permute-done | bytes 393248 | tf_op jit(solution)/shard_map/ppermute | solution.py:19
  87.2 7.0 %collective-permute-done.3 = f32[48,16,128]{2,0,1:T(8,128)} collective-permute-done((f32[48,16,128]{2,0,1:T(8,128)}, f32[48,16,128]{2,0,1:T(8,128)}, u32[]{:S(2)}, u32[]{:S(2)}) %collective-permute-start.3) | collective-permute-done | bytes 393248 | tf_op jit(solution)/shard_map/ppermute | solution.py:21
  94.2 2.5 %fusion.4 = f32[16,80,128]{2,0,1:T(8,128)S(1)} fusion(f32[48,16,128]{2,0,1:T(8,128)} %collective-permute-done.3, f32[48,48,128]{2,0,1:T(8,128)} %copy-done, f32[48,16,128]{2,0,1:T(8,128)S(1)} %collective-permute-done.2, f32[48,16]{1,0:T(8,128)} %get-tuple-element.6), kind=kOutput, calls=%fused_computation.6 | convolution fusion | flops 95354880 | bytes 2624512 | tf_op jit(solution)/shard_map/jyz,ji->iyz/dot_general | solution.py:92
  96.7 0.7 convolution_bitcast_fusion.1
  97.4 0.7 convolution_bitcast_fusion.3
  98.1 2.1 %fusion.5 = f32[16,80,128]{2,0,1:T(8,128)S(1)} fusion(f32[48,16,128]{2,0,1:T(8,128)} %collective-permute-done.3, f32[48,48,128]{2,0,1:T(8,128)S(1)} %copy-done.1, f32[48,16,128]{2,0,1:T(8,128)S(1)} %collective-permute-done.2, f32[48,16]{1,0:T(8,128)S(1)} %copy-done.6), kind=kOutput, calls=%fused_computation.7 | convolution fusion | flops 95354880 | bytes 2624512 | tf_op jit(solution)/shard_map/jyz,ji->iyz/dot_general | solution.py:93
  100.2 0.7 convolution_bitcast_fusion.5
  101.0 0.5 convolution_bitcast_fusion.2
  101.4 0.5 convolution_bitcast_fusion.4
  101.9 0.5 convolution_bitcast_fusion
  102.4 0.2 copy-done.4
  102.6 1.2 %fusion.7 = f32[3,16,48,128]{3,2,1,0:T(8,128)} fusion(f32[3,16,48,128]{3,2,1,0:T(8,128)S(1)} %copy-done.4, f32[3,16,48,128]{3,2,1,0:T(8,128)S(1)} %copy-done.2, f32[1,16,48,128]{3,2,1,0:T(8,128)S(1)} %convolution_bitcast_fusion, f32[1,16,48,128]{3,2,1,0:T(8,128)S(1)} %convolution_bitcast_fusion.2, f32[1,16,48,128]{3,2,1,0:T(8,128)S(1)} %convolution_bitcast_fusion.4, ...), kind=kLoop, calls=%fused_computation.16 | loop fusion | flops 1474560 | bytes 4718596 | tf_op jit(solution)/shard_map/add | solution.py:149
  (61 shorter events, 1.5 us)
Async XLA Ops:
  1.1 71.8 %collective-permute-start = (f32[16,48,128]{2,0,1:T(8,128)S(1)}, f32[16,48,128]{2,0,1:T(8,128)S(1)}, u32[]{:S(2)}, u32[]{:S(2)}) collective-permute-start(f32[16,48,128]{2,0,1:T(8,128)S(1)} %copy.182), channel_id=1, source_target_pairs={{0,4},{4,8},{8,12},{12,16},{16,20},{20,24},{24,28},{28,0},{1,5},{5... | collective-permute-start | bytes 1179656 | tf_op jit(solution)/shard_map/ppermute | solution.py:19
  1.7 71.4 %collective-permute-start.1 = (f32[16,48,128]{2,0,1:T(8,128)S(1)}, f32[16,48,128]{2,0,1:T(8,128)S(1)}, u32[]{:S(2)}, u32[]{:S(2)}) collective-permute-start(f32[16,48,128]{2,0,1:T(8,128)S(1)} %copy.182), channel_id=1, source_target_pairs={{4,0},{8,4},{12,8},{16,12},{20,16},{24,20},{28,24},{0,28},{5,1},{9... | collective-permute-start | bytes 1179656 | tf_op jit(solution)/shard_map/ppermute | solution.py:21
  36.4 6.3 %copy-start.11 = (f32[33]{0:T(128)S(1)}, f32[33]{0:T(128)}, u32[]{:S(2)}) copy-start(f32[33]{0:T(128)} %param.7) | copy-start | bytes 400
  37.2 6.5 %copy-start.10 = (f32[33]{0:T(128)S(1)}, f32[33]{0:T(128)}, u32[]{:S(2)}) copy-start(f32[33]{0:T(128)} %param.8) | copy-start | bytes 400
  38.8 9.2 %all-to-all-start = ((f32[8,1,1536]{2,1,0:T(1,128)}), f32[8,1,1536]{2,1,0:T(1,128)S(1)}, u32[]{:S(2)}, u32[]{:S(2)}) async-start(f32[8,1,1536]{2,1,0:T(1,128)} %reshape.222), calls=%async_computation | async-start | bytes 98304 | tf_op jit(solution)/shard_map/all_to_all | solution.py:128
  55.3 11.8 %all-to-all-start.1 = ((f32[8,1,4608]{2,1,0:T(1,128)}), f32[8,1,4608]{2,1,0:T(1,128)S(1)}, u32[]{:S(2)}, u32[]{:S(2)}) async-start(f32[8,1,4608]{2,1,0:T(1,128)} %reshape.224), calls=%async_computation.1 | async-start | bytes 294912 | tf_op jit(solution)/shard_map/all_to_all | solution.py:138
  69.1 3.9 %copy-start.3 = (f32[16,48,128]{2,1,0:T(8,128)S(1)}, f32[16,48,128]{2,1,0:T(8,128)}, u32[]{:S(2)}) copy-start(f32[16,48,128]{2,1,0:T(8,128)} %param.5) | copy-start | bytes 1179652
  73.1 4.7 %copy-start = (f32[48,48,128]{2,0,1:T(8,128)}, f32[48,48,128]{2,0,1:T(8,128)S(1)}, u32[]{:S(2)}) copy-start(f32[48,48,128]{2,0,1:T(8,128)S(1)} %constant_dynamic-update-slice_fusion) | copy-start | bytes 3538948
  74.1 13.1 %collective-permute-start.2 = (f32[48,16,128]{2,0,1:T(8,128)}, f32[48,16,128]{2,0,1:T(8,128)S(1)}, u32[]{:S(2)}, u32[]{:S(2)}) collective-permute-start(f32[48,16,128]{2,0,1:T(8,128)} %get-tuple-element.7), channel_id=1, source_target_pairs={{0,1},{1,2},{2,3},{3,0},{4,5},{5,6},{6,7},{7,4},{8,9},{9,10},{10,1... | collective-permute-start | bytes 1179656 | tf_op jit(solution)/shard_map/ppermute | solution.py:19
  75.5 18.7 %collective-permute-start.3 = (f32[48,16,128]{2,0,1:T(8,128)}, f32[48,16,128]{2,0,1:T(8,128)}, u32[]{:S(2)}, u32[]{:S(2)}) collective-permute-start(f32[48,16,128]{2,0,1:T(8,128)} %get-tuple-element.8), channel_id=1, source_target_pairs={{1,0},{2,1},{3,2},{0,3},{5,4},{6,5},{7,6},{4,7},{9,8},{10,9},{11,1... | collective-permute-start | bytes 1179656 | tf_op jit(solution)/shard_map/ppermute | solution.py:21
  94.2 2.5 %copy-start.7 = (f32[1,80,48]{1,0,2:T(1,128)S(1)}, f32[1,80,48]{1,0,2:T(1,128)}, u32[]{:S(2)}) copy-start(f32[1,80,48]{1,0,2:T(1,128)} %fusion.24) | copy-start | bytes 46084
  94.2 3.2 %copy-start.9 = (f32[1,80,48]{1,0,2:T(1,128)S(1)}, f32[1,80,48]{1,0,2:T(1,128)}, u32[]{:S(2)}) copy-start(f32[1,80,48]{1,0,2:T(1,128)} %fusion.23) | copy-start | bytes 46084
  96.7 1.4 %copy-start.1 = (f32[48,48,128]{2,0,1:T(8,128)S(1)}, f32[48,48,128]{2,0,1:T(8,128)}, u32[]{:S(2)}) copy-start(f32[48,48,128]{2,0,1:T(8,128)} %copy-done) | copy-start | bytes 3538948
  96.7 1.4 %copy-start.6 = (f32[48,16]{1,0:T(8,128)S(1)}, f32[48,16]{1,0:T(8,128)}, u32[]{:S(2)}) copy-start(f32[48,16]{1,0:T(8,128)} %get-tuple-element.5) | copy-start | bytes 9220
  98.1 2.8 %copy-start.5 = (f32[1,128,128]{2,0,1:T(1,128)S(1)}, f32[1,128,128]{2,0,1:T(1,128)}, u32[]{:S(2)}) copy-start(f32[1,128,128]{2,0,1:T(1,128)} %fusion.2) | copy-start | bytes 196612
  100.2 1.7 %copy-start.8 = (f32[1,128,128]{2,0,1:T(1,128)S(1)}, f32[1,128,128]{2,0,1:T(1,128)}, u32[]{:S(2)}) copy-start(f32[1,128,128]{2,0,1:T(1,128)} %fusion) | copy-start | bytes 196612
  100.9 1.4 %copy-start.2 = (f32[3,16,48,128]{3,2,1,0:T(8,128)S(1)}, f32[3,16,48,128]{3,2,1,0:T(8,128)}, u32[]{:S(2)}) copy-start(f32[3,16,48,128]{3,2,1,0:T(8,128)} %copy.216) | copy-start | bytes 3538948
  100.9 1.6 %copy-start.4 = (f32[3,16,48,128]{3,2,1,0:T(8,128)S(1)}, f32[3,16,48,128]{3,2,1,0:T(8,128)}, u32[]{:S(2)}) copy-start(f32[3,16,48,128]{3,2,1,0:T(8,128)} %param.6) | copy-start | bytes 3538948
